TPU v7x, 512 devices: a whole 4x4x16 slice. The times are simulated.
512 devices in a mesh: seq: 32 (over z, core), head: 16 (over x, y).
Axes of the slice: x: 4, y: 4, z: 16, core: 2. Of those that a mesh axis runs over, the one named last changes fastest.
Arguments:
- tokens: bfloat16 [8192, 4096], P('seq', 'head'), may hold values from -40 to 40
- norm_gain: float32 [4096], replicated, may hold values from 1.5 to 8
- w_qkv: bfloat16 [4096, 3, 2048], P(None, None, 'head'), may hold values from -0.09375 to 0.09375
- w_out: bfloat16 [2048, 4096], P('head'), may hold values from -0.75 to 0.75
- span_order: int32 [64], replicated, may hold values from 0 to 63, each once
- frame_id: int32 [8192], replicated, may hold values from 0 to 63, never falling along the last dimension, each value on 1 to 256 neighbouring positions
- camera_id: int32 [8192], replicated, may hold values from 0 to 5
Outputs:
- mixed: bfloat16 [8192, 4096], P('seq', 'head')
Inputs may be any that keep to these rules, and one draw needn't show every extreme that they name: `span_order`: each of the 64 spans appears once. `frame_id`: never falls along the sequence; every frame has 1 to 256 positions and one has exactly 256.
All inputs are finite; a program needn't handle non-finite values.
Results may differ from a plain program's by a relative error of at most 0.015.
The roundings to bfloat16 on the way count: a program that leaves them out, or rounds other values in their place, can miss the bound.
Values may be sent and summed in bfloat16 or wider, within the bound.
No kernel may reach another device: no remote copies, remote signals or barrier semaphores. Data moves between devices by JAX's collectives and lax.ppermute only.
A program may use at most 64 MiB of HBM per device.

v0:
```python
import jax
import jax.numpy as jnp
from jax import lax
from jax.sharding import PartitionSpec as P

D = 4096
HD = 128
epsilon = 1e-06
key_block = 1024


def stored_order(id_table, span_order):
    span_count = span_order.shape[0]
    return id_table.reshape(span_count, -1)[span_order].reshape(-1)


def visible_pairs(query_frames, query_cameras, key_frames, key_cameras):
    earlier = key_frames[None, :] < query_frames[:, None]
    same_view = (key_frames[None, :] == query_frames[:, None]) & (
        key_cameras[None, :] == query_cameras[:, None]
    )
    return earlier | same_view


def on_device(tokens, norm_gain, w_qkv, w_out, span_order, frame_id, camera_id):
    gathered = lax.all_gather(tokens, "head", axis=1, tiled=True)
    widened = gathered.astype(jnp.float32)
    inverse = lax.rsqrt(jnp.mean(widened * widened, axis=1, keepdims=True) + epsilon)
    normed = (widened * inverse * norm_gain).astype(jnp.bfloat16)
    row_count = tokens.shape[0]
    local_heads = w_out.shape[0] // HD
    projected = jnp.dot(
        normed, w_qkv.reshape(D, 3 * local_heads * HD), preferred_element_type=jnp.float32
    )
    projected = projected.astype(jnp.bfloat16).reshape(row_count, 3, local_heads, HD)
    queries = projected[:, 0]
    key_rows = projected[:, 1].reshape(row_count, local_heads * HD)
    value_rows = projected[:, 2].reshape(row_count, local_heads * HD)
    frames = stored_order(frame_id, span_order)
    cameras = stored_order(camera_id, span_order)
    first_row = lax.axis_index("seq") * row_count
    query_frames = lax.dynamic_slice_in_dim(frames, first_row, row_count, 0)
    query_cameras = lax.dynamic_slice_in_dim(cameras, first_row, row_count, 0)
    score_scale = HD ** (-0.5)

    def absorb(running, block_keys, block_values, key_start, frame_table, camera_table):
        key_count = block_keys.shape[0]
        key_frames = lax.dynamic_slice_in_dim(frame_table, key_start, key_count, 0)
        key_cameras = lax.dynamic_slice_in_dim(camera_table, key_start, key_count, 0)
        old_best, running_total, weighted = running
        scores = (
            jnp.einsum(
                "qhd,khd->hqk",
                queries,
                block_keys.reshape(key_count, local_heads, HD),
                preferred_element_type=jnp.float32,
            )
            * score_scale
        )
        allowed = visible_pairs(query_frames, query_cameras, key_frames, key_cameras)[None]
        block_best = jnp.max(jnp.where(allowed, scores, -jnp.inf), axis=2)
        new_best = jnp.maximum(old_best, block_best)
        weights = jnp.exp(jnp.where(allowed, scores - new_best[:, :, None], -jnp.inf))
        factor = jnp.exp(old_best - new_best)
        running_total = running_total * factor + jnp.sum(weights, axis=2)
        added = jnp.einsum(
            "hqk,khd->hqd",
            weights.astype(jnp.bfloat16),
            block_values.reshape(key_count, local_heads, HD),
            preferred_element_type=jnp.float32,
        )
        weighted = weighted * factor[:, :, None] + added
        return (new_best, running_total, weighted)

    initial = (
        jnp.full((local_heads, row_count), -1e30, jnp.float32),
        jnp.zeros((local_heads, row_count), jnp.float32),
        jnp.zeros((local_heads, row_count, HD), jnp.float32),
    )
    all_keys, all_values = (
        lax.all_gather(key_rows, "seq", axis=0, tiled=True),
        lax.all_gather(value_rows, "seq", axis=0, tiled=True),
    )
    running = initial
    length = all_keys.shape[0]
    block_rows = min(key_block, length)
    full_blocks = length // block_rows

    def advance(block_index, current):
        offset = block_index * block_rows
        block_keys = lax.dynamic_slice_in_dim(all_keys, offset, block_rows, 0)
        block_values = lax.dynamic_slice_in_dim(all_values, offset, block_rows, 0)
        return absorb(current, block_keys, block_values, 0 + offset, frames, cameras)

    running = lax.fori_loop(0, full_blocks, advance, running)
    attended = (running[2] / running[1][:, :, None]).astype(jnp.bfloat16)
    partial_value = jnp.einsum(
        "hqd,hde->qe",
        attended,
        w_out.reshape(local_heads, HD, D),
        preferred_element_type=jnp.float32,
    )
    mixed_rows = lax.psum_scatter(
        partial_value.astype(jnp.bfloat16), "head", scatter_dimension=1, tiled=True
    )
    return mixed_rows


def solution(mesh):
    placed = (P("seq", "head"), P(), P(None, None, "head"), P("head", None), P(), P(), P())
    return jax.shard_map(
        on_device, mesh=mesh, in_specs=placed, out_specs=P("seq", "head"), check_vma=False
    )
```

profile of v0, /device:TPU:2, one launch (start us, length us, event | category | flops | bytes accessed | tf_op | source)
XLA Modules:
  0.0 355.3 jit_solution(11500444099656653798)
XLA Ops:
  6.5 0.0 copy-start
  6.5 0.0 all-gather.6.cloned.1.call-start
  6.5 0.7 all-gather.6.cloned.1.call-update
  7.3 0.0 all-gather.10.cloned.1.call-start
  7.3 0.0 copy-start.4
  7.3 4.7 %copy.11 = bf16[4096,3,128]{0,2,1:T(8,128)(2,1)} copy(bf16[4096,3,128]{2,0,1:T(8,128)(2,1)} %param.11) | data formatting | bytes 6291456 | tf_op args[2]
  12.0 64.8 %all-gather.6.cloned.1.call-done = bf16[256,4096]{1,0:T(8,128)(2,1)} async-done(((bf16[256,256]{1,0:T(8,128)(2,1)}), bf16[256,4096]{1,0:T(8,128)(2,1)}) %all-gather.6.cloned.1.call-update) | async-done | bytes 2097168 | tf_op jit(solution)/shard_map/all_gather | solution.py:26
  76.8 0.0 copy-start.3
  76.8 2.2 fusion.16
  79.1 0.0 copy-done.4
  79.1 0.0 copy-done.3
  79.1 0.0 copy-start.5
  79.1 0.0 copy-start.1
  79.1 0.0 copy-start.2
  79.1 3.3 fusion.23
  82.4 0.1 copy.12
  82.6 0.7 fusion.27
  83.2 0.0 all-gather.10.cloned.1.call-update
  83.3 0.0 all-gather.8.cloned.1.call-start
  83.3 0.7 all-gather.8.cloned.1.call-update
  84.0 0.0 reduce-scatter.2.cloned.1.call-start
  84.1 0.0 copy-done.5
  84.1 0.0 copy-done.1
  84.1 0.6 gather_fusion.1
  84.7 0.0 copy-done.2
  84.7 0.6 gather_fusion
  85.3 0.1 dynamic_slice.35
  85.4 0.1 dynamic_slice.34
  85.5 0.1 copy.13
  85.6 70.4 %all-gather.10.cloned.1.call-done = bf16[8192,1,1,128]{0,3,1,2:T(8,128)(2,1)} async-done(((bf16[256,1,1,128]{0,3,1,2:T(8,128)(2,1)}), bf16[8192,1,1,128]{0,3,1,2:T(8,128)(2,1)}) %all-gather.10.cloned.1.call-update) | async-done | bytes 2097168 | tf_op jit(solution)/shard_map/all_gather | solution.py:82
  156.0 70.8 %all-gather.8.cloned.1.call-done = bf16[8192,1,1,128]{0,3,1,2:T(8,128)(2,1)} async-done(((bf16[256,1,1,128]{0,3,1,2:T(8,128)(2,1)}), bf16[8192,1,1,128]{0,3,1,2:T(8,128)(2,1)}) %all-gather.8.cloned.1.call-update) | async-done | bytes 2097168 | tf_op jit(solution)/shard_map/all_gather | solution.py:81
  226.8 33.6 %while.18 = (s32[]{:T(128)}, f32[1,256]{1,0:T(1,128)S(1)}, f32[1,256]{1,0:T(1,128)S(1)}, f32[1,256,128]{2,1,0:T(8,128)S(1)}, s32[8192]{0:T(1024)S(1)}, /*index=5...) while((s32[]{:T(128)}, f32[1,256]{1,0:T(1,128)S(1)}, ...), condition=%wide.region_4.5_spmd.clone, body=%wide.region_1.4_spmd.clone.sunk | while | flops 140608768 | bytes 4061407 | solution.py:95
  226.8 1.7 select_reduce_fusion.2
  228.6 0.7 fusion.39
  229.3 1.7 fusion.41
  231.0 1.8 select_reduce_fusion.2
  232.8 0.7 fusion.39
  233.5 1.7 fusion.41
  235.3 1.8 select_reduce_fusion.2
  237.0 0.7 fusion.39
  237.7 1.7 fusion.41
  239.5 1.8 select_reduce_fusion.2
  241.3 0.7 fusion.39
  242.0 1.7 fusion.41
  243.7 1.8 select_reduce_fusion.2
  245.5 0.7 fusion.39
  246.2 1.7 fusion.41
  247.9 1.8 select_reduce_fusion.2
  249.7 0.7 fusion.39
  250.4 1.7 fusion.41
  252.1 1.8 select_reduce_fusion.2
  253.9 0.7 fusion.39
  254.6 1.7 fusion.41
  256.3 1.8 select_reduce_fusion.2
  258.1 0.7 fusion.39
  258.8 1.7 fusion.41
  260.5 0.0 copy-done
  260.5 2.1 convolution_convert_fusion
  262.6 0.0 reduce-scatter.2.cloned.1.call-update
  262.6 86.2 %reduce-scatter.2.cloned.1.call-done = bf16[256,256]{1,0:T(8,128)(2,1)} async-done(((bf16[256,4096]{1,0:T(8,128)(2,1)}), bf16[256,256]{1,0:T(8,128)(2,1)}) %reduce-scatter.2.cloned.1.call-update) | async-done | bytes 131088 | tf_op jit(solution)/shard_map/reduce_scatter | solution.py:103
  (46 shorter events, 0.4 us)
Async XLA Ops:
  6.5 254.0 %copy-start = (bf16[128,4096]{1,0:T(8,128)(2,1)S(1)}, bf16[128,4096]{1,0:T(8,128)(2,1)}, u32[]{:S(2)}) copy-start(bf16[128,4096]{1,0:T(8,128)(2,1)} %param.12) | copy-start | bytes 3145732
  6.5 70.3 %all-gather.6.cloned.1.call-start = ((), (), s32[]{:S(2)}) async-start(), calls=%async_computation.1 | async-start | bytes 2228224 | tf_op jit(solution)/shard_map/all_gather | solution.py:26
  7.3 148.8 %all-gather.10.cloned.1.call-start = ((), (), s32[]{:S(2)}) async-start(), calls=%async_computation.4 | async-start | bytes 2162688 | tf_op jit(solution)/shard_map/all_gather | solution.py:82
  7.3 71.7 %copy-start.4 = (f32[4096]{0:T(1024)S(1)}, f32[4096]{0:T(1024)}, u32[]{:S(2)}) copy-start(f32[4096]{0:T(1024)} %param.10) | copy-start | bytes 49156
  76.8 2.3 copy-start.3
  79.1 5.0 %copy-start.5 = (s32[64]{0:T(128)S(1)}, s32[64]{0:T(128)}, u32[]{:S(2)}) copy-start(s32[64]{0:T(128)} %param.13) | copy-start | bytes 772
  79.1 5.0 %copy-start.1 = (s32[8192]{0:T(1024)S(1)}, s32[8192]{0:T(1024)}, u32[]{:S(2)}) copy-start(s32[8192]{0:T(1024)} %param.15) | copy-start | bytes 98308
  79.1 5.6 %copy-start.2 = (s32[8192]{0:T(1024)S(1)}, s32[8192]{0:T(1024)}, u32[]{:S(2)}) copy-start(s32[8192]{0:T(1024)} %param.14) | copy-start | bytes 98308
  83.3 143.6 %all-gather.8.cloned.1.call-start = ((), (), s32[]{:S(2)}) async-start(), calls=%async_computation.3 | async-start | bytes 2162688 | tf_op jit(solution)/shard_map/all_gather | solution.py:81
  84.0 264.8 %reduce-scatter.2.cloned.1.call-start = ((), (), s32[]{:S(2)}) async-start(), calls=%async_computation.2 | async-start | bytes 2228224 | tf_op jit(solution)/shard_map/reduce_scatter | solution.py:103
Sparse Core Ops, SparseCore 0:
  10.3 66.4 all-gather.5
  83.4 72.6 all-gather.9
  158.1 68.7 all-gather.7
  262.7 86.0 reduce-scatter.1
where the time goes:
time: 356 us; the launch traced here: 355 us
  waiting for transfers between devices  294 us (83%)
  matrix products  32.7 us (9%)
  between operations  13.3 us (4%)
  other arithmetic  7.89 us (2%)
  local copies, waits for them, and re-layouts  7.13 us (2%)
    reduce_scatter x1, waiting for transfers between devices, on_device(): lax.psum_scatter(partial_value.astype(jnp.bfloat16), 'head', scatter_dime...  86.2 us
    all_gather x1, waiting for transfers between devices, on_device(): lax.all_gather(key_rows, 'seq', axis=0, tiled=True)  70.8 us
    all_gather x1, waiting for transfers between devices, on_device(): lax.all_gather(value_rows, 'seq', axis=0, tiled=True)  70.4 us
    all_gather x1, waiting for transfers between devices, on_device(): gathered = lax.all_gather(tokens, 'head', axis=1, tiled=True)  64.8 us
    dot_general x8, matrix products, absorb(): jnp.einsum('qhd,khd->hqk', queries, block_keys.reshape(key_count, local_h...  14.1 us
    dot_general x8, matrix products, absorb(): jnp.einsum('hqk,khd->hqd', weights.astype(jnp.bfloat16), block_values.res...  13.2 us
  transfers between devices with their start and end apart: 4, of which 4 were waited for; matrix products, arithmetic and copies ran while one was open for 2% of the time, Pallas kernels for 0%

commit v1 on v0

--- a/solution.py
+++ b/solution.py
@@ -23,7 +23,7 @@
 
 
 def on_device(tokens, norm_gain, w_qkv, w_out, span_order, frame_id, camera_id):
-    gathered = lax.all_gather(tokens, "head", axis=1, tiled=True)
+    gathered = jnp.concatenate(lax.all_gather(tokens, "head"), axis=1)
     widened = gathered.astype(jnp.float32)
     inverse = lax.rsqrt(jnp.mean(widened * widened, axis=1, keepdims=True) + epsilon)
     normed = (widened * inverse * norm_gain).astype(jnp.bfloat16)

time: 356 us -> 357 us (level)
  no operation moved by 1% of the time
where the time goes in v1:
time: 357 us
  waiting for transfers between devices  291 us (82%)
  matrix products  33.2 us (9%)
  between operations  13.2 us (4%)
  local copies, waits for them, and re-layouts  10.2 us (3%)
  other arithmetic  8.51 us (2%)
    reduce_scatter x1, waiting for transfers between devices, on_device(): lax.psum_scatter(partial_value.astype(jnp.bfloat16), 'head', scatter_dime...  86.3 us
    all_gather x1, waiting for transfers between devices, on_device(): lax.all_gather(key_rows, 'seq', axis=0, tiled=True)  70.8 us
    all_gather x1, waiting for transfers between devices, on_device(): lax.all_gather(value_rows, 'seq', axis=0, tiled=True)  70.4 us
    all_gather x1, waiting for transfers between devices, on_device(): gathered = jnp.concatenate(lax.all_gather(tokens, 'head'), axis=1)  62 us
    dot_general x8, matrix products, absorb(): jnp.einsum('qhd,khd->hqk', queries, block_keys.reshape(key_count, local_h...  14.1 us
    dot_general x8, matrix products, absorb(): jnp.einsum('hqk,khd->hqd', weights.astype(jnp.bfloat16), block_values.res...  13.2 us
  transfers between devices with their start and end apart: 4, of which 4 were waited for; matrix products, arithmetic and copies ran while one was open for 2% of the time, Pallas kernels for 0%

profile of v1, /device:TPU:2, one launch (start us, length us, event | category | flops | bytes accessed | tf_op | source)
XLA Modules:
  0.0 356.8 jit_solution(1341115986836770903)
XLA Ops:
  6.5 0.0 copy-start
  6.5 0.0 all-gather.7.cloned.1.call-start
  6.5 0.7 all-gather.7.cloned.1.call-update
  7.3 0.0 all-gather.11.cloned.1.call-start
  7.3 0.7 mul.81
  8.0 4.7 %copy.17 = bf16[4096,3,128]{0,2,1:T(8,128)(2,1)} copy(bf16[4096,3,128]{2,0,1:T(8,128)(2,1)} %param.11) | data formatting | bytes 6291456 | tf_op args[2]
  12.7 62.0 %all-gather.7.cloned.1.call-done = bf16[4096,256]{1,0:T(8,128)(2,1)} async-done(((bf16[256,256]{1,0:T(8,128)(2,1)}), bf16[4096,256]{1,0:T(8,128)(2,1)}) %all-gather.7.cloned.1.call-update) | async-done | bytes 2097168 | tf_op jit(solution)/shard_map/all_gather | solution.py:26
  74.7 0.0 copy-start.1
  74.7 2.2 fusion.16
  77.0 0.0 copy-done.1
  77.0 0.6 fusion.19
  77.6 2.4 copy.16
  80.0 0.0 copy-start.4
  80.0 0.0 copy-start.2
  80.0 0.0 copy-start.3
  80.0 3.8 %convolution_convert_fusion.1 = bf16[256,384]{1,0:T(8,128)(2,1)S(1)} fusion(bf16[256,4096]{0,1:T(8,128)(2,1)} %bitcast.53, bf16[4096,384]{0,1:T(8,128)(2,1)} %bitcast.50), kind=kOutput, calls=%fused_computation.33 | convolution fusion | flops 805404672 | bytes 5439488 | tf_op jit(solution)/shard_map/dot_general | solution.py:32
  83.8 0.1 copy.18
  84.0 0.7 fusion.21
  84.6 0.0 all-gather.11.cloned.1.call-update
  84.7 0.0 all-gather.9.cloned.1.call-start
  84.7 0.7 all-gather.9.cloned.1.call-update
  85.4 0.0 reduce-scatter.2.cloned.1.call-start
  85.5 0.0 copy-done.4
  85.5 0.0 copy-done.2
  85.5 0.6 gather_fusion.1
  86.1 0.0 copy-done.3
  86.1 0.6 gather_fusion
  86.7 0.1 dynamic_slice.35
  86.8 0.1 dynamic_slice.34
  86.9 0.1 copy.19
  87.0 70.4 %all-gather.11.cloned.1.call-done = bf16[8192,1,1,128]{0,3,1,2:T(8,128)(2,1)} async-done(((bf16[256,1,1,128]{0,3,1,2:T(8,128)(2,1)}), bf16[8192,1,1,128]{0,3,1,2:T(8,128)(2,1)}) %all-gather.11.cloned.1.call-update) | async-done | bytes 2097168 | tf_op jit(solution)/shard_map/all_gather | solution.py:82
  157.4 70.8 %all-gather.9.cloned.1.call-done = bf16[8192,1,1,128]{0,3,1,2:T(8,128)(2,1)} async-done(((bf16[256,1,1,128]{0,3,1,2:T(8,128)(2,1)}), bf16[8192,1,1,128]{0,3,1,2:T(8,128)(2,1)}) %all-gather.9.cloned.1.call-update) | async-done | bytes 2097168 | tf_op jit(solution)/shard_map/all_gather | solution.py:81
  228.2 33.6 %while.18 = (s32[]{:T(128)}, f32[1,256]{1,0:T(1,128)S(1)}, f32[1,256]{1,0:T(1,128)S(1)}, f32[1,256,128]{2,1,0:T(8,128)S(1)}, s32[8192]{0:T(1024)S(1)}, /*index=5...) while((s32[]{:T(128)}, f32[1,256]{1,0:T(1,128)S(1)}, ...), condition=%wide.region_4.5_spmd.clone, body=%wide.region_1.4_spmd.clone.sunk | while | flops 140608768 | bytes 4061407 | solution.py:95
  228.2 1.7 select_reduce_fusion.2
  230.0 0.7 fusion.34
  230.7 1.7 fusion.36
  232.4 1.8 select_reduce_fusion.2
  234.2 0.7 fusion.34
  234.9 1.7 fusion.36
  236.6 1.8 select_reduce_fusion.2
  238.4 0.7 fusion.34
  239.1 1.7 fusion.36
  240.9 1.8 select_reduce_fusion.2
  242.6 0.7 fusion.34
  243.3 1.7 fusion.36
  245.1 1.8 select_reduce_fusion.2
  246.9 0.7 fusion.34
  247.6 1.7 fusion.36
  249.3 1.8 select_reduce_fusion.2
  251.1 0.7 fusion.34
  251.8 1.7 fusion.36
  253.5 1.8 select_reduce_fusion.2
  255.3 0.7 fusion.34
  256.0 1.7 fusion.36
  257.7 1.8 select_reduce_fusion.2
  259.5 0.7 fusion.34
  260.2 1.7 fusion.36
  261.9 0.0 copy-done
  261.9 2.1 convolution_convert_fusion
  264.0 0.0 reduce-scatter.2.cloned.1.call-update
  264.0 86.3 %reduce-scatter.2.cloned.1.call-done = bf16[256,256]{1,0:T(8,128)(2,1)} async-done(((bf16[256,4096]{1,0:T(8,128)(2,1)}), bf16[256,256]{1,0:T(8,128)(2,1)}) %reduce-scatter.2.cloned.1.call-update) | async-done | bytes 131088 | tf_op jit(solution)/shard_map/reduce_scatter | solution.py:103
  (46 shorter events, 0.4 us)
Async XLA Ops:
  6.5 255.3 %copy-start = (bf16[128,4096]{1,0:T(8,128)(2,1)S(1)}, bf16[128,4096]{1,0:T(8,128)(2,1)}, u32[]{:S(2)}) copy-start(bf16[128,4096]{1,0:T(8,128)(2,1)} %param.12) | copy-start | bytes 3145732
  6.5 68.2 %all-gather.7.cloned.1.call-start = ((), (), s32[]{:S(2)}) async-start(), calls=%async_computation.2 | async-start | bytes 2228224 | tf_op jit(solution)/shard_map/all_gather | solution.py:26
  7.3 150.2 %all-gather.11.cloned.1.call-start = ((), (), s32[]{:S(2)}) async-start(), calls=%async_computation.4 | async-start | bytes 2162688 | tf_op jit(solution)/shard_map/all_gather | solution.py:82
  74.7 2.2 copy-start.1
  80.0 5.5 %copy-start.4 = (s32[64]{0:T(128)S(1)}, s32[64]{0:T(128)}, u32[]{:S(2)}) copy-start(s32[64]{0:T(128)} %param.13) | copy-start | bytes 772
  80.0 5.5 %copy-start.2 = (s32[8192]{0:T(1024)S(1)}, s32[8192]{0:T(1024)}, u32[]{:S(2)}) copy-start(s32[8192]{0:T(1024)} %param.15) | copy-start | bytes 98308
  80.0 6.1 %copy-start.3 = (s32[8192]{0:T(1024)S(1)}, s32[8192]{0:T(1024)}, u32[]{:S(2)}) copy-start(s32[8192]{0:T(1024)} %param.14) | copy-start | bytes 98308
  84.7 143.6 %all-gather.9.cloned.1.call-start = ((), (), s32[]{:S(2)}) async-start(), calls=%async_computation.3 | async-start | bytes 2162688 | tf_op jit(solution)/shard_map/all_gather | solution.py:81
  85.4 264.9 %reduce-scatter.2.cloned.1.call-start = ((), (), s32[]{:S(2)}) async-start(), calls=%async_computation.1 | async-start | bytes 2228224 | tf_op jit(solution)/shard_map/reduce_scatter | solution.py:103
Sparse Core Ops, SparseCore 0:
  10.3 64.3 all-gather.6
  84.8 72.5 all-gather.10
  159.5 68.7 all-gather.8
  264.1 86.1 reduce-scatter.1
